TPU v7x, 128 devices: a whole 4x4x4 slice. The times are simulated.
128 devices in a mesh: seq: 64 (over y_lo, x, z, core), ch: 2 (over y_hi).
Axes of the slice: x: 4, y: 4 (y_hi: 2, y_lo: 2; y = y_hi * 2 + y_lo), z: 4, core: 2. Of those that a mesh axis runs over, the one named last changes fastest.
Arguments:
- out_grad: bfloat16 [8192, 4096], P('seq', 'ch'), may hold values from -6 to 6
- out_weight: bfloat16 [4096, 4096], P(('seq', 'ch')), may hold values from -0.09375 to 0.09375
- outer_gate: bfloat16 [8192, 4096], P('seq', 'ch'), may hold values from -6 to 6
- long_out: bfloat16 [8192, 4096], P('seq', 'ch'), may hold values from -6 to 6
- inner_gate: bfloat16 [8192, 4096], P('seq', 'ch'), may hold values from -6 to 6
- conv_input: bfloat16 [8192, 4096], P('seq', 'ch'), may hold values from -6 to 6
- short_out: bfloat16 [8192, 4096], P('seq', 'ch'), may hold values from -6 to 6
- medium_out: bfloat16 [8192, 4096], P('seq', 'ch'), may hold values from -6 to 6
- long_filter: bfloat16 [8192, 4096], P('seq', 'ch'), may hold values from -6 to 6
- taps_short: bfloat16 [7, 4096], P(None, 'ch'), may hold values from -2 to 2
- taps_medium: bfloat16 [128, 4096], P(None, 'ch'), may hold values from -0.5 to 0.5
Outputs:
- grad_outer: bfloat16 [8192, 4096], P('seq', 'ch')
- grad_inner: bfloat16 [8192, 4096], P('seq', 'ch')
- grad_input: bfloat16 [8192, 4096], P('seq', 'ch')
- grad_filter: float32 [8192, 4096], P('seq', 'ch')
- grad_short: float32 [7, 4096], P(None, 'ch')
- grad_medium: float32 [128, 4096], P(None, 'ch')
All inputs are finite; a program needn't handle non-finite values.
Results may differ from a plain program's by a relative error of at most 0.0065.
Values may be sent and summed in bfloat16 or wider, within the bound.
A program may use at most 128 MiB of HBM per device.

v0:
```python
import math
import jax
import jax.numpy as jnp
from jax import lax
from jax.sharding import PartitionSpec as P

SHORT = 7
MEDIUM = 128
ACCURATE = lax.Precision.HIGH


def from_behind(value, axis, steps):
    count = lax.axis_size(axis)
    leading, last = (max(0, -steps), min(count, count - steps))
    return lax.ppermute(value, axis, [(source, source + steps) for source in range(leading, last)])


def in_order(parts, dim):
    parts = jnp.moveaxis(parts, 0, dim)
    shape = parts.shape
    return parts.reshape(*shape[:dim], shape[dim] * shape[dim + 1], *shape[dim + 2 :])


def sent_to_all(x, axis):
    size = lax.axis_size(axis)
    return lax.all_to_all(jnp.broadcast_to(x[None], (size, *x.shape)), axis, 0, 0, tiled=True)


def gathered_copies(x, axis, dim):
    return in_order(sent_to_all(x, axis), dim)


def side_by_side(arrays, axis, split_dim, concat_dim, along):
    ends, at = ([], 0)
    for a in arrays[:-1]:
        at += a.shape[along]
        ends.append(at)
    both = jnp.concatenate(arrays, axis=along)
    return tuple(
        jnp.split(
            lax.all_to_all(both, axis, split_axis=split_dim, concat_axis=concat_dim, tiled=True),
            ends,
            axis=along,
        )
    )


def padded_to(lines, size):
    spare = -lines.shape[0] % size
    if not spare:
        return lines
    return jnp.concatenate([lines, jnp.zeros((spare, *lines.shape[1:]), lines.dtype)])


def cut_along(x, dim, size):
    before, after = (x.shape[:dim], x.shape[dim + 1 :])
    return jnp.moveaxis(x.reshape(*before, size, -1, *after), dim, 0)


def summed_on_arrival(x, axis, dim):
    size = lax.axis_size(axis)
    parts = lax.all_to_all(cut_along(x, dim, size), axis, 0, 0, tiled=True)
    return jnp.sum(parts.astype(jnp.float32), axis=0)


def total_of(x, axes):
    lines = x.reshape(-1)
    padded = padded_to(lines, lax.axis_size(axes))
    whole = gathered_copies(summed_on_arrival(padded, axes, 0).astype(jnp.bfloat16), axes, 0)
    return lax.slice_in_dim(whole, 0, len(lines)).reshape(x.shape).astype(jnp.float32)


def rotation(numer, denom):
    angles = 2.0 * math.pi / denom * numer.astype(jnp.float32)
    return (jnp.cos(angles), jnp.sin(angles))


def dft_table(length, orient):
    indices = lax.iota(jnp.int32, length)
    cosine, sine_part = rotation(indices[:, None] * indices[None, :] % length, length)
    return (cosine, orient * sine_part)


def apply_table(table, real_part, imag_part, pattern):

    def multiply(left, right):
        return jnp.einsum(pattern, left, right, precision=ACCURATE)

    if imag_part is None:
        return (multiply(table[0], real_part), multiply(table[1], real_part))
    return (
        multiply(table[0], real_part) - multiply(table[1], imag_part),
        multiply(table[0], imag_part) + multiply(table[1], real_part),
    )


def real_table(table, real_part, imag_part, pattern):
    return jnp.einsum(pattern, table[0], real_part, precision=ACCURATE) - jnp.einsum(
        pattern, table[1], imag_part, precision=ACCURATE
    )


def twist(real_part, imag_part, cosine, sine_part):
    return (real_part * cosine - imag_part * sine_part, real_part * sine_part + imag_part * cosine)


def outer_forward(signal, time_pos, row_pos, freq_pos, total):
    table = dft_table(signal.shape[0], -1.0)
    cosine, sine_part = rotation(time_pos, 2 * total)
    shift_real, shift_imag = rotation(row_pos * freq_pos % total, total)
    outputs = []
    for parity in range(2):
        if parity == 0:
            real_part, imag_part = apply_table(table, signal, None, "ca,am->cm")
        else:
            real_part, imag_part = apply_table(
                table, signal * cosine, -signal * sine_part, "ca,am->cm"
            )
        outputs += list(twist(real_part, imag_part, shift_real, -shift_imag))
    return outputs


def inner_forward(parts):
    table = dft_table(parts[0].shape[0], -1.0)
    outputs = []
    for place in range(0, len(parts), 2):
        outputs += list(apply_table(table, parts[place], parts[place + 1], "br,rn->bn"))
    return outputs


def inner_inverse(parts, narrow, total):
    table = dft_table(parts[0].shape[0], 1.0)
    row_pos = lax.iota(jnp.int32, parts[0].shape[0])[:, None]
    freq_pos = lax.iota(jnp.int32, parts[0].shape[1])[None, :] // narrow
    shift_real, shift_imag = rotation(row_pos * freq_pos % total, total)
    outputs = []
    for place in range(0, len(parts), 2):
        real_part, imag_part = apply_table(table, parts[place], parts[place + 1], "rb,bn->rn")
        outputs += list(twist(real_part, imag_part, shift_real, shift_imag))
    return outputs


def outer_inverse(parts, time_pos, total):
    table = dft_table(parts[0].shape[0], 1.0)
    cosine, sine_part = rotation(time_pos, 2 * total)
    outputs = []
    for place in range(0, len(parts), 4):
        high_real, high_imag = apply_table(table, parts[place + 2], parts[place + 3], "ac,cm->am")
        high_real, high_imag = twist(high_real, high_imag, cosine, sine_part)
        outputs.append(real_table(table, parts[place], parts[place + 1], "ac,cm->am") + high_real)
    return outputs


def conj_times(left_real, left_imag, right_real, right_imag):
    return (
        left_real * right_real + left_imag * right_imag,
        left_real * right_imag - left_imag * right_real,
    )


def spectral_terms(spectra):
    first, second = ([], [])
    for parity in range(2):
        grad_real, grad_imag = (spectra[4 + 2 * parity], spectra[5 + 2 * parity])
        point_real, point_imag = conj_times(
            spectra[8 + 2 * parity], spectra[9 + 2 * parity], grad_real, grad_imag
        )
        filt_real, filt_imag = conj_times(
            spectra[2 * parity], spectra[2 * parity + 1], grad_real, grad_imag
        )
        first += [point_real, point_imag]
        second += [filt_real, filt_imag]
    return first + second


def depthwise(signal, kernel):
    channels = signal.shape[1]
    result = lax.conv_general_dilated(
        signal.astype(jnp.float32)[None],
        kernel.astype(jnp.float32)[:, None, :],
        (1,),
        "VALID",
        dimension_numbers=("NWC", "WIO", "NWC"),
        feature_group_count=channels,
        precision=lax.Precision.HIGHEST,
    )
    return result[0]


def adjoint_taps(extended, taps):
    return depthwise(extended, taps)


def tap_products(grads, extended):
    return depthwise(extended, grads)[::-1]


def per_device(
    out_grad,
    out_weight,
    outer_gate,
    long_out,
    inner_gate,
    conv_input,
    short_out,
    medium_out,
    long_filter,
    taps_short,
    taps_medium,
):
    height = out_grad.shape[0]
    channels = outer_gate.shape[1]
    devices = lax.axis_size("seq")
    total = height * devices
    earlier_short, earlier_input = from_behind(
        (short_out[height - (MEDIUM - 1) :], conv_input[height - (SHORT - 1) :]), "seq", 1
    )
    features = gathered_copies(out_grad, "ch", 1)
    aligned = lax.all_to_all(out_weight, "ch", split_axis=1, concat_axis=0, tiled=True)
    hidden = jnp.dot(
        features,
        lax.all_gather(aligned, "seq", axis=0, tiled=True),
        preferred_element_type=jnp.float32,
    )
    grad_outer = (hidden * long_out.astype(jnp.float32)).astype(jnp.bfloat16)
    long_grad = (hidden * outer_gate.astype(jnp.float32)).astype(jnp.bfloat16)
    product = (inner_gate.astype(jnp.float32) * medium_out.astype(jnp.float32)).astype(jnp.bfloat16)
    narrow = channels // devices
    lane_span = height * narrow

    def to_blocks(signal):
        return (
            signal.reshape(height, devices, narrow).transpose(1, 0, 2).reshape(devices, lane_span)
        )

    def to_inner(signal):
        return (
            signal.reshape(devices, height, narrow)
            .transpose(1, 0, 2)
            .reshape(height, devices * narrow)
        )

    arrived = side_by_side(
        (to_blocks(product), to_blocks(long_grad), to_blocks(long_filter)), "seq", 0, 0, 1
    )
    row_pos = lax.iota(jnp.int32, lane_span)[None, :] // narrow
    source = lax.iota(jnp.int32, devices)[:, None]
    time_pos = source * height + row_pos
    spread = []
    for signal in arrived:
        spread += outer_forward(signal.astype(jnp.float32), time_pos, row_pos, source, total)
    spectra = inner_forward([to_inner(piece) for piece in spread])
    terms = inner_inverse(spectral_terms(spectra), narrow, total)
    results = outer_inverse([to_blocks(piece) for piece in terms], time_pos, total)
    result = lax.all_to_all(jnp.stack(results), "seq", split_axis=1, concat_axis=1, tiled=True)
    result = (
        result.reshape(2, devices, height, narrow)
        .transpose(0, 2, 1, 3)
        .reshape(2, height, channels)
    )
    scale = total ** (-0.5) / (2.0 * total)
    point_grad = result[0] * scale
    grad_filter = result[1] * scale
    medium_grad = (point_grad * inner_gate.astype(jnp.float32)).astype(jnp.bfloat16)
    grad_inner = (point_grad * medium_out.astype(jnp.float32)).astype(jnp.bfloat16)
    later_medium = from_behind(medium_grad[: MEDIUM - 1], "seq", -1)
    short_grad = adjoint_taps(jnp.concatenate([medium_grad, later_medium]), taps_medium).astype(
        jnp.bfloat16
    )
    later_short = from_behind(short_grad[: SHORT - 1], "seq", -1)
    grad_input = adjoint_taps(jnp.concatenate([short_grad, later_short]), taps_short).astype(
        jnp.bfloat16
    )
    partial_medium = tap_products(medium_grad, jnp.concatenate([earlier_short, short_out]))
    partial_short = tap_products(short_grad, jnp.concatenate([earlier_input, conv_input]))
    sum_medium, sum_short = (
        total_of(partial_medium.astype(jnp.bfloat16), "seq"),
        total_of(partial_short.astype(jnp.bfloat16), "seq"),
    )
    factor = total ** (-0.5)
    return (
        grad_outer,
        grad_inner,
        grad_input,
        grad_filter,
        sum_short * factor,
        sum_medium * factor,
    )


def solution(mesh):
    return jax.shard_map(
        per_device,
        mesh=mesh,
        in_specs=(
            P("seq", "ch"),
            P(("seq", "ch"), None),
            P("seq", "ch"),
            P("seq", "ch"),
            P("seq", "ch"),
            P("seq", "ch"),
            P("seq", "ch"),
            P("seq", "ch"),
            P("seq", "ch"),
            P(None, "ch"),
            P(None, "ch"),
        ),
        out_specs=(
            P("seq", "ch"),
            P("seq", "ch"),
            P("seq", "ch"),
            P("seq", "ch"),
            P(None, "ch"),
            P(None, "ch"),
        ),
        check_vma=False,
    )
```

profile of v0, /device:TPU:1, one launch (start us, length us, event | category | flops | bytes accessed | tf_op | source)
XLA Modules:
  0.0 697.4 jit_solution(6125251082649983839)
XLA Ops:
  8.2 10.4 %all_to_all.73 = bf16[32,2,2048]{2,0,1:T(8,128)(2,1)} all-to-all(bf16[32,2,2048]{2,0,1:T(8,128)(2,1)S(1)} %bitcast.295), channel_id=1, replica_groups=mesh['seq'=64,'ch'=2] {'ch'}, dimensions={1} | all-to-all | bytes 524288 | tf_op jit(solution)/shard_map/all_to_all | solution.py:219
  32.0 5.8 all-to-all-done
  37.8 109.5 %all-gather.2.cloned.1.call-done = bf16[4096,2048]{1,0:T(8,128)(2,1)} async-done(((bf16[64,2048]{1,0:T(8,128)(2,1)}), bf16[4096,2048]{1,0:T(8,128)(2,1)}) %all-gather.2.cloned.1.call-update) | async-done | bytes 16777232 | tf_op jit(solution)/shard_map/all_gather | solution.py:222
  147.2 9.3 %multiply_convert_fusion = (bf16[128,2048]{1,0:T(8,128)(2,1)}, bf16[128,2048]{1,0:T(8,128)(2,1)}) fusion(bf16[128,2048]{1,0:T(8,128)(2,1)} %param.13, bf16[128,2048]{1,0:T(8,128)(2,1)} %param.14, bf16[128,4096]{0,1:T(8,128)(2,1)S(1)} %bitcast.274, bf16[4096,2048]{1,0:T(8,128)(2,1)} %all-gather.2.cloned.1.call-done), kind=kOutput, calls=%fused_computation.128 | convolution fusion | flops 2149056512 | bytes 19922944 | tf_op jit(solution)/shard_map/dot_general | solution.py:220
  162.5 13.1 %maximum_bitcast_fusion = bf16[64,1,12288]{0,2,1:T(8,128)(2,1)} fusion(bf16[64,4096]{0,1:T(8,128)(2,1)S(1)} %bitcast.286, bf16[64,4096]{0,1:T(8,128)(2,1)} %bitcast.288, bf16[64,4096]{0,1:T(8,128)(2,1)S(1)} %bitcast.287), kind=kLoop, calls=%fused_computation.22 | loop fusion | flops 4718592 | bytes 3145728 | tf_op jit(solution)/shard_map/all_to_all | solution.py:41
  176.1 5.6 reduce.8
  186.9 6.5 all-to-all-start.2
  193.4 22.6 %all-to-all-done.2 = bf16[64,2,6144]{2,1,0:T(2,128)(2,1)S(1)} async-done(((bf16[64,2,6144]{2,1,0:T(2,128)(2,1)}), bf16[64,2,6144]{2,1,0:T(2,128)(2,1)S(1)}, u32[]{:S(2)}, u32[]{:S(2)}) %all-to-all-start.2) | async-done | bytes 1572896 | tf_op jit(solution)/shard_map/all_to_all | solution.py:41
  243.5 4.6 fusion.41
  278.0 8.8 %multiply_subtract_fusion.13 = (f32[64,4096]{1,0:T(8,128)}, f32[64,4096]{1,0:T(8,128)}, f32[64,4096]{1,0:T(8,128)S(1)}, f32[64,4096]{1,0:T(8,128)S(1)}, f32[64,4...) fusion(f32[64,4096]{1,0:T(8,128)S(1)} %fusion.118, ...), kind=kOutput, calls=%fused_computation.124 | convolution fusion | flops 114094080 | bytes 24657920 | tf_op jit(solution)/shard_map/ca,am->cm/dot_general | solution.py:87
  410.6 7.7 %multiply_add_fusion.10 = (f32[128,2048]{1,0:T(8,128)}, f32[128,2048]{1,0:T(8,128)}, f32[128,2048]{1,0:T(8,128)}, f32[128,2048]{1,0:T(8,128)}, f32[128,2048]{1,0...) fusion(f32[128,2048]{1,0:T(8,128)S(1)} %copy-done.17, ...), kind=kOutput, calls=%fused_computation.115 | convolution fusion | flops 211779584 | bytes 17833984 | tf_op jit(solution)/shard_map/rb,bn->rn/dot_general | solution.py:87
  433.0 6.6 fusion
  466.8 6.3 fusion.4
  487.9 7.4 %fusion.9 = f32[64,4096]{1,0:T(8,128)S(1)} fusion(f32[64,4096]{1,0:T(8,128)} %fusion, f32[64,4096]{1,0:T(8,128)} %fusion.207, f32[64,4096]{0,1:T(8,128)S(1)} %bitcast.229, s32[64]{0:T(128)S(1)} %iota_multiply_fusion, s32[4096]{0:T(1024)S(1)} %add_select_fusion.4), kind=kOutput, calls=%fused_computation.21 | convolution fusion | flops 102293504 | bytes 4210944 | tf_op jit(solution)/shard_map/ac,cm->am/dot_general | solution.py:87
  506.3 5.5 all-to-all-start.3
  516.6 24.1 %collective-permute-done.3 = bf16[127,2048]{1,0:T(8,128)(2,1)S(1)} collective-permute-done((bf16[127,2048]{1,0:T(8,128)(2,1)S(1)}, bf16[127,2048]{1,0:T(8,128)(2,1)S(1)}, u32[]{:S(2)}, u32[]{:S(2)}) %collective-permute-start.3) | collective-permute-done | bytes 520224 | tf_op jit(solution)/shard_map/ppermute | solution.py:15
  556.1 16.4 %fusion.11 = bf16[1,128,2048]{2,0,1:T(2,128)(2,1)S(1)} fusion(bf16[128,1,2048]{2,1,0:T(2,128)(2,1)S(1)} %copy.365, bf16[1,255,2048]{2,1,0:T(8,128)(2,1)} %maximum_bitcast_fusion.2), kind=kOutput, calls=%fused_computation.47 | convolution fusion | flops 67108864 | bytes 2093056 | tf_op jit(solution)/shard_map/conv_general_dilated | solution.py:178
  579.4 10.4 %all-to-all-start.6 = ((bf16[64,2,2048]{2,1,0:T(2,128)(2,1)}), bf16[64,2,2048]{2,1,0:T(2,128)(2,1)S(1)}, u32[]{:S(2)}, u32[]{:S(2)}) async-start(bf16[64,2,2048]{2,1,0:T(2,128)(2,1)} %reshape.352), calls=%async_computation.6 | async-start | bytes 1048576 | tf_op jit(solution)/shard_map/all_to_all | solution.py:62
  614.7 17.4 %convolution_convert_fusion = bf16[1,128,2048]{2,0,1:T(2,128)(2,1)S(1)} fusion(bf16[1,255,2048]{2,0,1:T(2,128)(2,1)} %copy.355, bf16[128,1,2048]{2,0,1:T(8,128)(2,1)S(1)} %bitcast.205), kind=kOutput, calls=%fused_computation.44 | convolution fusion | flops 67371008 | bytes 2093056 | tf_op jit(solution)/shard_map/conv_general_dilated | solution.py:178
  638.6 8.3 %all-to-all-start.4 = ((bf16[64,1,224]{2,1,0:T(2,128)(2,1)}), bf16[64,1,224]{2,1,0:T(2,128)(2,1)S(1)}, u32[]{:S(2)}, u32[]{:S(2)}) async-start(bf16[64,1,224]{2,1,0:T(2,128)(2,1)} %all_to_all.63), calls=%async_computation.4 | async-start | bytes 131072 | tf_op jit(solution)/shard_map/all_to_all | solution.py:62
  647.6 7.5 %all-to-all-done.4 = bf16[64,1,224]{2,1,0:T(2,128)(2,1)S(1)} async-done(((bf16[64,1,224]{2,1,0:T(2,128)(2,1)}), bf16[64,1,224]{2,1,0:T(2,128)(2,1)S(1)}, u32[]{:S(2)}, u32[]{:S(2)}) %all-to-all-start.4) | async-done | bytes 28704 | tf_op jit(solution)/shard_map/all_to_all | solution.py:62
  661.7 7.0 all-to-all-done.5
  668.6 4.7 all-to-all-start.7
  675.1 10.3 %all-to-all-done.7 = bf16[64,2,2048]{2,1,0:T(2,128)(2,1)S(1)} async-done(((bf16[64,2,2048]{2,1,0:T(2,128)(2,1)}), bf16[64,2,2048]{2,1,0:T(2,128)(2,1)S(1)}, u32[]{:S(2)}, u32[]{:S(2)}) %all-to-all-start.7) | async-done | bytes 524320 | tf_op jit(solution)/shard_map/all_to_all | solution.py:26
  (298 shorter events, 345.9 us)
Async XLA Ops:
  7.2 607.5 %copy-start = (bf16[128,2048]{1,0:T(8,128)(2,1)S(1)}, bf16[128,2048]{1,0:T(8,128)(2,1)}, u32[]{:S(2)}) copy-start(bf16[128,2048]{1,0:T(8,128)(2,1)} %param.21) | copy-start | bytes 1572868
  7.2 140.0 %all-gather.2.cloned.1.call-start = ((), (), s32[]{:S(2)}) async-start(), calls=%async_computation.8 | async-start | bytes 17039360 | tf_op jit(solution)/shard_map/all_gather | solution.py:222
  21.1 16.7 %all-to-all-start = ((bf16[2,128,2048]{1,2,0:T(8,128)(2,1)}), bf16[2,128,2048]{1,2,0:T(8,128)(2,1)S(1)}, u32[]{:S(2)}, u32[]{:S(2)}) async-start(bf16[2,128,2048]{1,2,0:T(8,128)(2,1)} %broadcast_in_dim.20), calls=%async_computation | async-start | bytes 2097152 | tf_op jit(solution)/shard_map/all_to_all | solution.py:26
  29.2 127.4 %copy-start.15 = (bf16[128,2048]{0,1:T(8,128)(2,1)}, bf16[128,2048]{0,1:T(8,128)(2,1)S(1)}, u32[]{:S(2)}) copy-start(bf16[128,2048]{0,1:T(8,128)(2,1)S(1)} %copy.304) | copy-start | bytes 1572868
  156.6 5.9 copy-start.35
  156.6 5.9 copy-start.36
  186.9 29.2 %all-to-all-start.2 = ((bf16[64,2,6144]{2,1,0:T(2,128)(2,1)}), bf16[64,2,6144]{2,1,0:T(2,128)(2,1)S(1)}, u32[]{:S(2)}, u32[]{:S(2)}) async-start(bf16[64,2,6144]{2,1,0:T(2,128)(2,1)} %reshape.350), calls=%async_computation.2 | async-start | bytes 3145728 | tf_op jit(solution)/shard_map/all_to_all | solution.py:41
  487.9 7.4 %copy-start.4 = (f32[64,128,32]{0,2,1:T(8,128)S(1)}, f32[64,128,32]{0,2,1:T(8,128)}, u32[]{:S(2)}) copy-start(f32[64,128,32]{0,2,1:T(8,128)} %copy-done.3) | copy-start | bytes 3145732
  487.9 7.4 %copy-start.32 = (f32[64,4096]{1,0:T(8,128)S(1)}, f32[64,4096]{1,0:T(8,128)}, u32[]{:S(2)}) copy-start(f32[64,4096]{1,0:T(8,128)} %fusion.216) | copy-start | bytes 3145732
  487.9 7.4 %copy-start.33 = (f32[64,4096]{1,0:T(8,128)S(1)}, f32[64,4096]{1,0:T(8,128)}, u32[]{:S(2)}) copy-start(f32[64,4096]{1,0:T(8,128)} %fusion.4) | copy-start | bytes 3145732
  506.3 36.5 %all-to-all-start.3 = ((f32[2,64,4096]{2,0,1:T(2,128)}), f32[2,64,4096]{2,0,1:T(2,128)S(1)}, u32[]{:S(2)}, u32[]{:S(2)}) async-start(f32[2,64,4096]{2,0,1:T(2,128)} %copy.351), calls=%async_computation.3 | async-start | bytes 4194304 | tf_op jit(solution)/shard_map/all_to_all | solution.py:255
  513.0 27.6 %collective-permute-start.3 = (bf16[127,2048]{1,0:T(8,128)(2,1)S(1)}, bf16[127,2048]{1,0:T(8,128)(2,1)S(1)}, u32[]{:S(2)}, u32[]{:S(2)}) collective-permute-start(bf16[127,2048]{1,0:T(8,128)(2,1)S(1)} %slice.29), channel_id=1, source_target_pairs={{0,2},{2,4},{4,6},{6,8},{8,10},{10,12},{12,14},{14,16},{16,18},{18... | collective-permute-start | bytes 1560584 | tf_op jit(solution)/shard_map/ppermute | solution.py:15
  553.2 56.2 %collective-permute-start = (bf16[127,2048]{0,1:T(8,128)(2,1)S(1)}, bf16[127,2048]{0,1:T(8,128)(2,1)}, u32[]{:S(2)}, u32[]{:S(2)}) collective-permute-start(bf16[127,2048]{0,1:T(8,128)(2,1)S(1)} %bitcast.275), channel_id=1, source_target_pairs={{2,0},{4,2},{6,4},{8,6},{10,8},{12,10},{14,12},{16,14},{18,16},{20... | collective-permute-start | bytes 1560584 | tf_op jit(solution)/shard_map/ppermute | solution.py:15
  574.3 23.3 %copy-start.51 = (bf16[128,2048]{0,1:T(8,128)(2,1)S(1)}, bf16[128,2048]{0,1:T(8,128)(2,1)}, u32[]{:S(2)}) copy-start(bf16[128,2048]{0,1:T(8,128)(2,1)} %get-tuple-element.71) | copy-start | bytes 1572868
  578.2 20.4 %copy-start.34 = (f32[1,128,64,32]{1,3,2,0:T(8,128)S(1)}, f32[1,128,64,32]{1,3,2,0:T(8,128)}, u32[]{:S(2)}) copy-start(f32[1,128,64,32]{1,3,2,0:T(8,128)} %get-tuple-element.64) | copy-start | bytes 3145732
  579.4 22.3 %all-to-all-start.6 = ((bf16[64,2,2048]{2,1,0:T(2,128)(2,1)}), bf16[64,2,2048]{2,1,0:T(2,128)(2,1)S(1)}, u32[]{:S(2)}, u32[]{:S(2)}) async-start(bf16[64,2,2048]{2,1,0:T(2,128)(2,1)} %reshape.352), calls=%async_computation.6 | async-start | bytes 1048576 | tf_op jit(solution)/shard_map/all_to_all | solution.py:62
  590.6 5.1 collective-permute-start.2
  614.7 19.9 %copy-start.52 = (bf16[1,134,2048]{2,1,0:T(8,128)(2,1)S(1)}, bf16[1,134,2048]{2,1,0:T(8,128)(2,1)}, u32[]{:S(2)}) copy-start(bf16[1,134,2048]{2,1,0:T(8,128)(2,1)} %maximum_bitcast_fusion.4) | copy-start | bytes 1646596
  632.2 14.7 %collective-permute-start.1 = (bf16[6,2048]{1,0:T(8,128)(2,1)S(1)}, bf16[6,2048]{1,0:T(8,128)(2,1)S(1)}, u32[]{:S(2)}, u32[]{:S(2)}) collective-permute-start(bf16[6,2048]{1,0:T(8,128)(2,1)S(1)} %bitcast.298), channel_id=1, source_target_pairs={{2,0},{4,2},{6,4},{8,6},{10,8},{12,10},{14,12},{16,14},{18,16},{20... | collective-permute-start | bytes 73736 | tf_op jit(solution)/shard_map/ppermute | solution.py:15
  638.6 16.5 %all-to-all-start.4 = ((bf16[64,1,224]{2,1,0:T(2,128)(2,1)}), bf16[64,1,224]{2,1,0:T(2,128)(2,1)S(1)}, u32[]{:S(2)}, u32[]{:S(2)}) async-start(bf16[64,1,224]{2,1,0:T(2,128)(2,1)} %all_to_all.63), calls=%async_computation.4 | async-start | bytes 131072 | tf_op jit(solution)/shard_map/all_to_all | solution.py:62
  647.0 13.4 %copy-start.55 = (bf16[7,2048]{1,0:T(8,128)(2,1)S(1)}, bf16[7,2048]{1,0:T(8,128)(2,1)}, u32[]{:S(2)}) copy-start(bf16[7,2048]{1,0:T(8,128)(2,1)} %param.20) | copy-start | bytes 86020
  647.0 13.4 %copy-start.56 = (pred[8,17]{0,1:T(8,128)(4,1)S(1)}, pred[8,17]{0,1:T(8,128)(4,1)}, u32[]{:S(2)}) copy-start(pred[8,17]{0,1:T(8,128)(4,1)} %constant.132) | copy-start | bytes 412
  655.9 12.8 %all-to-all-start.5 = ((bf16[64,1,224]{2,1,0:T(2,128)(2,1)}), bf16[64,1,224]{2,1,0:T(2,128)(2,1)S(1)}, u32[]{:S(2)}, u32[]{:S(2)}) async-start(bf16[64,1,224]{2,1,0:T(2,128)(2,1)} %broadcast_in_dim.26), calls=%async_computation.5 | async-start | bytes 131072 | tf_op jit(solution)/shard_map/all_to_all | solution.py:26
  668.6 16.8 %all-to-all-start.7 = ((bf16[64,2,2048]{2,1,0:T(2,128)(2,1)}), bf16[64,2,2048]{2,1,0:T(2,128)(2,1)S(1)}, u32[]{:S(2)}, u32[]{:S(2)}) async-start(bf16[64,2,2048]{2,1,0:T(2,128)(2,1)} %reshape.354), calls=%async_computation.7 | async-start | bytes 1048576 | tf_op jit(solution)/shard_map/all_to_all | solution.py:26
  (45 other events, 117.7 us)
Sparse Core Ops, SparseCore 0:
  18.8 128.3 all-gather.1
where the time goes:
time: 706 us; the launch traced here: 697 us
  matrix products  212 us (30%)
  waiting for transfers between devices  190 us (27%)
  local copies, waits for them, and re-layouts  175 us (25%)
  starting transfers between devices  54.8 us (8%)
  other arithmetic  39 us (6%)
  between operations  15.6 us (2%)
  blocking collectives  10.4 us (1%)
    dot_general x66, matrix products, multiply(): return jnp.einsum(pattern, left, right, precision=ACCURATE)  158 us
    all_gather x1, waiting for transfers between devices, per_device(): lax.all_gather(aligned, 'seq', axis=0, tiled=True)  109 us
    transpose x12, local copies, waits for them, and re-layouts, to_inner(): return signal.reshape(devices, height, narrow).transpose(1, 0, 2).reshape...  37.1 us
    conv_general_dilated x4, matrix products, depthwise(): lax.conv_general_dilated(signal.astype(jnp.float32)[None], kernel.astype(...  37.1 us
    transpose x11, local copies, waits for them, and re-layouts, to_blocks(): signal.reshape(height, devices, narrow).transpose(1, 0, 2)  34.3 us
    unnamed x132, local copies, waits for them, and re-layouts  27.5 us
    ppermute x4, waiting for transfers between devices, from_behind(): lax.ppermute(value, axis, [(source, source + steps) for source in range(l...  25.6 us
    sub x10, local copies, waits for them, and re-layouts, twist(): real_part * cosine - imag_part * sine_part  24.4 us
  transfers between devices with their start and end apart: 12, of which 9 were waited for; matrix products, arithmetic and copies ran while one was open for 8% of the time, Pallas kernels for 0%

commit v1 on v0

--- a/solution.py
+++ b/solution.py
@@ -219,7 +219,9 @@
     aligned = lax.all_to_all(out_weight, "ch", split_axis=1, concat_axis=0, tiled=True)
     hidden = jnp.dot(
         features,
-        lax.all_gather(aligned, "seq", axis=0, tiled=True),
+        jnp.concatenate(
+            lax.all_to_all(jnp.stack([aligned] * lax.axis_size("seq")), "seq", 0, 0), axis=0
+        ),
         preferred_element_type=jnp.float32,
     )
     grad_outer = (hidden * long_out.astype(jnp.float32)).astype(jnp.bfloat16)

time: 706 us -> 844 us (1.20)
  waiting for transfers between devices: 190 us -> 291 us
  starting transfers between devices: 54.8 us -> 94.2 us
  between operations: 15.6 us -> 2.22 us
    all_to_all x0 -> x2, waiting for transfers between devices: none -> 216 us  [the longest x1 212 us: per_device(): lax.all_to_all(jnp.stack([aligned] * lax.axis_size('seq')), 'seq', 0, 0)]
    all_gather x1 -> x0, waiting for transfers between devices: 109 us -> none  [per_device(): lax.all_gather(aligned, 'seq', axis=0, tiled=True)]
    all_to_all x1, starting transfers between devices: 6.52 us -> 32.3 us  [side_by_side(): lax.all_to_all(both, axis, split_axis=split_dim, concat_axis=concat_dim,...]
    all_to_all x0 -> x2, starting transfers between devices: none -> 17.3 us  [the longest x1 12.3 us: per_device(): lax.all_to_all(jnp.stack([aligned] * lax.axis_size('seq')), 'seq', 0, 0)]
    all_to_all x3 -> x2, waiting for transfers between devices: 23.1 us -> 17.3 us  [sent_to_all(): lax.all_to_all(jnp.broadcast_to(x[None], (size, *x.shape)), axis, 0, 0, t...]
  transfers between devices with their start and end apart: 12 -> 12, of which waited for: 9 -> 9; matrix products, arithmetic and copies ran while one was open for 8% -> 7% of each run, Pallas kernels for 0% -> 0%
where the time goes in v1:
time: 844 us; the launch traced here: 835 us
  waiting for transfers between devices  291 us (34%)
  matrix products  212 us (25%)
  local copies, waits for them, and re-layouts  181 us (21%)
  starting transfers between devices  94.2 us (11%)
  other arithmetic  39 us (5%)
  blocking collectives  15.5 us (2%)
    all_to_all x1, waiting for transfers between devices, per_device(): lax.all_to_all(jnp.stack([aligned] * lax.axis_size('seq')), 'seq', 0, 0)  212 us
    dot_general x66, matrix products, multiply(): return jnp.einsum(pattern, left, right, precision=ACCURATE)  158 us
    transpose x12, local copies, waits for them, and re-layouts, to_inner(): return signal.reshape(devices, height, narrow).transpose(1, 0, 2).reshape...  37.1 us
    conv_general_dilated x4, matrix products, depthwise(): lax.conv_general_dilated(signal.astype(jnp.float32)[None], kernel.astype(...  37.1 us
    transpose x11, local copies, waits for them, and re-layouts, to_blocks(): signal.reshape(height, devices, narrow).transpose(1, 0, 2)  34.3 us
    all_to_all x1, starting transfers between devices, side_by_side(): lax.all_to_all(both, axis, split_axis=split_dim, concat_axis=concat_dim,...  32.3 us
    unnamed x132, local copies, waits for them, and re-layouts  27.5 us
    ppermute x4, waiting for transfers between devices, from_behind(): lax.ppermute(value, axis, [(source, source + steps) for source in range(l...  25.6 us
  transfers between devices with their start and end apart: 12, of which 9 were waited for; matrix products, arithmetic and copies ran while one was open for 7% of the time, Pallas kernels for 0%

profile of v1, /device:TPU:1, one launch (start us, length us, event | category | flops | bytes accessed | tf_op | source)
XLA Modules:
  0.0 835.0 jit_solution(6393189606294344681)
XLA Ops:
  2.4 5.0 all-to-all-start.1
  13.0 15.5 %all_to_all.75 = bf16[2,128,2048]{1,2,0:T(8,128)(2,1)S(1)} all-to-all(bf16[2,128,2048]{1,2,0:T(8,128)(2,1)S(1)} %broadcast_in_dim.20), channel_id=1, replica_groups=mesh['seq'=64,'ch'=2] {'ch'}, dimensions={0} | all-to-all | bytes 2097152 | tf_op jit(solution)/shard_map/all_to_all | solution.py:26
  28.5 5.9 stack.11
  34.5 12.3 %all-to-all-start.2 = ((bf16[64,64,2048]{2,1,0:T(8,128)(2,1)}), bf16[64,64,2048]{2,1,0:T(8,128)(2,1)}, u32[]{:S(2)}, u32[]{:S(2)}) async-start(bf16[64,64,2048]{2,1,0:T(8,128)(2,1)} %stack.11), calls=%async_computation.2 | async-start | bytes 33554432 | tf_op jit(solution)/shard_map/all_to_all | solution.py:223
  54.0 211.7 %all-to-all-done.2 = bf16[64,64,2048]{2,1,0:T(8,128)(2,1)} async-done(((bf16[64,64,2048]{2,1,0:T(8,128)(2,1)}), bf16[64,64,2048]{2,1,0:T(8,128)(2,1)}, u32[]{:S(2)}, u32[]{:S(2)}) %all-to-all-start.2) | async-done | bytes 16777248 | tf_op jit(solution)/shard_map/all_to_all | solution.py:223
  265.8 9.4 %multiply_convert_fusion = (bf16[128,2048]{1,0:T(8,128)(2,1)}, bf16[128,2048]{1,0:T(8,128)(2,1)}) fusion(bf16[128,2048]{1,0:T(8,128)(2,1)} %param.13, bf16[128,2048]{1,0:T(8,128)(2,1)} %param.14, bf16[128,4096]{0,1:T(8,128)(2,1)S(1)} %bitcast.275, bf16[4096,2048]{1,0:T(8,128)(2,1)} %bitcast.4), kind=kOutput, calls=%fused_computation.128 | convolution fusion | flops 2149056512 | bytes 19922944 | tf_op jit(solution)/shard_map/dot_general | solution.py:220
  281.0 13.1 %maximum_bitcast_fusion = bf16[64,1,12288]{0,2,1:T(8,128)(2,1)} fusion(bf16[64,4096]{0,1:T(8,128)(2,1)S(1)} %bitcast.287, bf16[64,4096]{0,1:T(8,128)(2,1)} %bitcast.289, bf16[64,4096]{0,1:T(8,128)(2,1)S(1)} %bitcast.288), kind=kLoop, calls=%fused_computation.22 | loop fusion | flops 4718592 | bytes 3145728 | tf_op jit(solution)/shard_map/all_to_all | solution.py:41
  294.6 5.6 reduce.8
  305.4 32.3 %all-to-all-start.3 = ((bf16[64,2,6144]{2,1,0:T(2,128)(2,1)}), bf16[64,2,6144]{2,1,0:T(2,128)(2,1)S(1)}, u32[]{:S(2)}, u32[]{:S(2)}) async-start(bf16[64,2,6144]{2,1,0:T(2,128)(2,1)} %reshape.357), calls=%async_computation.3 | async-start | bytes 3145728 | tf_op jit(solution)/shard_map/all_to_all | solution.py:41
  337.8 22.6 %all-to-all-done.3 = bf16[64,2,6144]{2,1,0:T(2,128)(2,1)S(1)} async-done(((bf16[64,2,6144]{2,1,0:T(2,128)(2,1)}), bf16[64,2,6144]{2,1,0:T(2,128)(2,1)S(1)}, u32[]{:S(2)}, u32[]{:S(2)}) %all-to-all-start.3) | async-done | bytes 1572896 | tf_op jit(solution)/shard_map/all_to_all | solution.py:41
  422.4 8.8 %multiply_subtract_fusion.13 = (f32[64,4096]{1,0:T(8,128)}, f32[64,4096]{1,0:T(8,128)}, f32[64,4096]{1,0:T(8,128)S(1)}, f32[64,4096]{1,0:T(8,128)S(1)}, f32[64,4...) fusion(f32[64,4096]{1,0:T(8,128)S(1)} %fusion.118, ...), kind=kOutput, calls=%fused_computation.124 | convolution fusion | flops 114094080 | bytes 24657920 | tf_op jit(solution)/shard_map/ca,am->cm/dot_general | solution.py:87
  555.0 7.7 multiply_add_fusion.10
  577.4 6.6 fusion
  611.4 6.3 fusion.4
  632.4 7.4 fusion.9
  650.8 5.5 all-to-all-start.4
  661.0 24.1 %collective-permute-done.3 = bf16[127,2048]{1,0:T(8,128)(2,1)S(1)} collective-permute-done((bf16[127,2048]{1,0:T(8,128)(2,1)S(1)}, bf16[127,2048]{1,0:T(8,128)(2,1)S(1)}, u32[]{:S(2)}, u32[]{:S(2)}) %collective-permute-start.3) | collective-permute-done | bytes 520224 | tf_op jit(solution)/shard_map/ppermute | solution.py:15
  700.5 16.4 %fusion.11 = bf16[1,128,2048]{2,0,1:T(2,128)(2,1)S(1)} fusion(bf16[128,1,2048]{2,1,0:T(2,128)(2,1)S(1)} %copy.365, bf16[1,255,2048]{2,1,0:T(8,128)(2,1)} %maximum_bitcast_fusion.2), kind=kOutput, calls=%fused_computation.47 | convolution fusion | flops 67108864 | bytes 2093056 | tf_op jit(solution)/shard_map/conv_general_dilated | solution.py:178
  723.8 10.4 %all-to-all-start.7 = ((bf16[64,2,2048]{2,1,0:T(2,128)(2,1)}), bf16[64,2,2048]{2,1,0:T(2,128)(2,1)S(1)}, u32[]{:S(2)}, u32[]{:S(2)}) async-start(bf16[64,2,2048]{2,1,0:T(2,128)(2,1)} %reshape.359), calls=%async_computation.7 | async-start | bytes 1048576 | tf_op jit(solution)/shard_map/all_to_all | solution.py:62
  759.1 17.4 %convolution_convert_fusion = bf16[1,128,2048]{2,0,1:T(2,128)(2,1)S(1)} fusion(bf16[1,255,2048]{2,0,1:T(2,128)(2,1)} %copy.355, bf16[128,1,2048]{2,0,1:T(8,128)(2,1)S(1)} %bitcast.206), kind=kOutput, calls=%fused_computation.44 | convolution fusion | flops 67371008 | bytes 2093056 | tf_op jit(solution)/shard_map/conv_general_dilated | solution.py:178
  783.0 8.3 all-to-all-start.5
  792.1 7.5 all-to-all-done.5
  806.1 7.0 all-to-all-done.6
  819.5 10.3 %all-to-all-done.8 = bf16[64,2,2048]{2,1,0:T(2,128)(2,1)S(1)} async-done(((bf16[64,2,2048]{2,1,0:T(2,128)(2,1)}), bf16[64,2,2048]{2,1,0:T(2,128)(2,1)S(1)}, u32[]{:S(2)}, u32[]{:S(2)}) %all-to-all-start.8) | async-done | bytes 524320 | tf_op jit(solution)/shard_map/all_to_all | solution.py:26
  (298 shorter events, 355.7 us)
Async XLA Ops:
  0.6 758.5 %copy-start = (bf16[128,2048]{1,0:T(8,128)(2,1)S(1)}, bf16[128,2048]{1,0:T(8,128)(2,1)}, u32[]{:S(2)}) copy-start(bf16[128,2048]{1,0:T(8,128)(2,1)} %param.21) | copy-start | bytes 1572868
  2.4 10.5 %all-to-all-start.1 = ((bf16[32,2,2048]{2,0,1:T(8,128)(2,1)}), bf16[32,2,2048]{2,0,1:T(8,128)(2,1)S(1)}, u32[]{:S(2)}, u32[]{:S(2)}) async-start(bf16[32,2,2048]{2,0,1:T(8,128)(2,1)} %bitcast.202), calls=%async_computation.1 | async-start | bytes 524288 | tf_op jit(solution)/shard_map/all_to_all | solution.py:219
  34.5 12.3 %copy-start.53 = (bf16[128,2048]{1,0:T(8,128)(2,1)S(1)}, bf16[128,2048]{1,0:T(8,128)(2,1)}, u32[]{:S(2)}) copy-start(bf16[128,2048]{1,0:T(8,128)(2,1)} %param.15) | copy-start | bytes 1572868
  34.5 12.6 %copy-start.54 = (bf16[128,2048]{1,0:T(8,128)(2,1)S(1)}, bf16[128,2048]{1,0:T(8,128)(2,1)}, u32[]{:S(2)}) copy-start(bf16[128,2048]{1,0:T(8,128)(2,1)} %param.19) | copy-start | bytes 1572868
  34.5 231.3 %all-to-all-start.2 = ((bf16[64,64,2048]{2,1,0:T(8,128)(2,1)}), bf16[64,64,2048]{2,1,0:T(8,128)(2,1)}, u32[]{:S(2)}, u32[]{:S(2)}) async-start(bf16[64,64,2048]{2,1,0:T(8,128)(2,1)} %stack.11), calls=%async_computation.2 | async-start | bytes 33554432 | tf_op jit(solution)/shard_map/all_to_all | solution.py:223
  51.3 223.9 %copy-start.15 = (bf16[128,2048]{0,1:T(8,128)(2,1)}, bf16[128,2048]{0,1:T(8,128)(2,1)S(1)}, u32[]{:S(2)}) copy-start(bf16[128,2048]{0,1:T(8,128)(2,1)S(1)} %copy.304) | copy-start | bytes 1572868
  305.4 55.0 %all-to-all-start.3 = ((bf16[64,2,6144]{2,1,0:T(2,128)(2,1)}), bf16[64,2,6144]{2,1,0:T(2,128)(2,1)S(1)}, u32[]{:S(2)}, u32[]{:S(2)}) async-start(bf16[64,2,6144]{2,1,0:T(2,128)(2,1)} %reshape.357), calls=%async_computation.3 | async-start | bytes 3145728 | tf_op jit(solution)/shard_map/all_to_all | solution.py:41
  632.4 7.4 copy-start.4
  632.4 7.4 copy-start.32
  632.4 7.4 copy-start.33
  650.8 36.5 %all-to-all-start.4 = ((f32[2,64,4096]{2,0,1:T(2,128)}), f32[2,64,4096]{2,0,1:T(2,128)S(1)}, u32[]{:S(2)}, u32[]{:S(2)}) async-start(f32[2,64,4096]{2,0,1:T(2,128)} %copy.351), calls=%async_computation.4 | async-start | bytes 4194304 | tf_op jit(solution)/shard_map/all_to_all | solution.py:257
  657.5 27.6 %collective-permute-start.3 = (bf16[127,2048]{1,0:T(8,128)(2,1)S(1)}, bf16[127,2048]{1,0:T(8,128)(2,1)S(1)}, u32[]{:S(2)}, u32[]{:S(2)}) collective-permute-start(bf16[127,2048]{1,0:T(8,128)(2,1)S(1)} %slice.29), channel_id=1, source_target_pairs={{0,2},{2,4},{4,6},{6,8},{8,10},{10,12},{12,14},{14,16},{16,18},{18... | collective-permute-start | bytes 1560584 | tf_op jit(solution)/shard_map/ppermute | solution.py:15
  697.7 56.2 %collective-permute-start = (bf16[127,2048]{0,1:T(8,128)(2,1)S(1)}, bf16[127,2048]{0,1:T(8,128)(2,1)}, u32[]{:S(2)}, u32[]{:S(2)}) collective-permute-start(bf16[127,2048]{0,1:T(8,128)(2,1)S(1)} %bitcast.276), channel_id=1, source_target_pairs={{2,0},{4,2},{6,4},{8,6},{10,8},{12,10},{14,12},{16,14},{18,16},{20... | collective-permute-start | bytes 1560584 | tf_op jit(solution)/shard_map/ppermute | solution.py:15
  718.8 23.3 %copy-start.51 = (bf16[128,2048]{0,1:T(8,128)(2,1)S(1)}, bf16[128,2048]{0,1:T(8,128)(2,1)}, u32[]{:S(2)}) copy-start(bf16[128,2048]{0,1:T(8,128)(2,1)} %get-tuple-element.71) | copy-start | bytes 1572868
  722.6 20.4 %copy-start.34 = (f32[1,128,64,32]{1,3,2,0:T(8,128)S(1)}, f32[1,128,64,32]{1,3,2,0:T(8,128)}, u32[]{:S(2)}) copy-start(f32[1,128,64,32]{1,3,2,0:T(8,128)} %get-tuple-element.64) | copy-start | bytes 3145732
  723.8 22.3 %all-to-all-start.7 = ((bf16[64,2,2048]{2,1,0:T(2,128)(2,1)}), bf16[64,2,2048]{2,1,0:T(2,128)(2,1)S(1)}, u32[]{:S(2)}, u32[]{:S(2)}) async-start(bf16[64,2,2048]{2,1,0:T(2,128)(2,1)} %reshape.359), calls=%async_computation.7 | async-start | bytes 1048576 | tf_op jit(solution)/shard_map/all_to_all | solution.py:62
  735.0 5.1 collective-permute-start.2
  759.1 19.9 %copy-start.52 = (bf16[1,134,2048]{2,1,0:T(8,128)(2,1)S(1)}, bf16[1,134,2048]{2,1,0:T(8,128)(2,1)}, u32[]{:S(2)}) copy-start(bf16[1,134,2048]{2,1,0:T(8,128)(2,1)} %maximum_bitcast_fusion.4) | copy-start | bytes 1646596
  776.6 14.7 %collective-permute-start.1 = (bf16[6,2048]{1,0:T(8,128)(2,1)S(1)}, bf16[6,2048]{1,0:T(8,128)(2,1)S(1)}, u32[]{:S(2)}, u32[]{:S(2)}) collective-permute-start(bf16[6,2048]{1,0:T(8,128)(2,1)S(1)} %bitcast.298), channel_id=1, source_target_pairs={{2,0},{4,2},{6,4},{8,6},{10,8},{12,10},{14,12},{16,14},{18,16},{20... | collective-permute-start | bytes 73736 | tf_op jit(solution)/shard_map/ppermute | solution.py:15
  783.0 16.5 %all-to-all-start.5 = ((bf16[64,1,224]{2,1,0:T(2,128)(2,1)}), bf16[64,1,224]{2,1,0:T(2,128)(2,1)S(1)}, u32[]{:S(2)}, u32[]{:S(2)}) async-start(bf16[64,1,224]{2,1,0:T(2,128)(2,1)} %all_to_all.64), calls=%async_computation.5 | async-start | bytes 131072 | tf_op jit(solution)/shard_map/all_to_all | solution.py:62
  791.4 13.4 %copy-start.55 = (bf16[7,2048]{1,0:T(8,128)(2,1)S(1)}, bf16[7,2048]{1,0:T(8,128)(2,1)}, u32[]{:S(2)}) copy-start(bf16[7,2048]{1,0:T(8,128)(2,1)} %param.20) | copy-start | bytes 86020
  791.4 13.4 %copy-start.56 = (pred[8,17]{0,1:T(8,128)(4,1)S(1)}, pred[8,17]{0,1:T(8,128)(4,1)}, u32[]{:S(2)}) copy-start(pred[8,17]{0,1:T(8,128)(4,1)} %constant.132) | copy-start | bytes 412
  800.3 12.8 %all-to-all-start.6 = ((bf16[64,1,224]{2,1,0:T(2,128)(2,1)}), bf16[64,1,224]{2,1,0:T(2,128)(2,1)S(1)}, u32[]{:S(2)}, u32[]{:S(2)}) async-start(bf16[64,1,224]{2,1,0:T(2,128)(2,1)} %broadcast_in_dim.26), calls=%async_computation.6 | async-start | bytes 131072 | tf_op jit(solution)/shard_map/all_to_all | solution.py:26
  813.1 16.8 %all-to-all-start.8 = ((bf16[64,2,2048]{2,1,0:T(2,128)(2,1)}), bf16[64,2,2048]{2,1,0:T(2,128)(2,1)S(1)}, u32[]{:S(2)}, u32[]{:S(2)}) async-start(bf16[64,2,2048]{2,1,0:T(2,128)(2,1)} %reshape.361), calls=%async_computation.8 | async-start | bytes 1048576 | tf_op jit(solution)/shard_map/all_to_all | solution.py:26
  (45 other events, 120.0 us)
